TPU v7x, 32 devices: a whole 2x2x4 slice. The times are simulated.
32 devices in a mesh: cam: 2 (over core), tile: 16 (over z, y, x).
Axes of the slice: x: 2, y: 2, z: 4, core: 2. Of those that a mesh axis runs over, the one named last changes fastest.
Arguments:
- queries: bfloat16 [4096, 256], P('tile'), as said below
- keys: bfloat16 [2048, 256], P(('cam', 'tile')), as said below
- values: bfloat16 [2048, 256], P(('cam', 'tile')), may hold values from -6 to 6
- grad_out: bfloat16 [4096, 256], P('tile'), may hold values from -6 to 6
- visible: int32 [32, 64], P('tile', 'cam'), may hold values from 0 to 1, as said below
- counts: int32 [64], P('cam'), may hold values from 2 to 32
Outputs:
- grad_queries: bfloat16 [4096, 256], P('tile')
- grad_keys: bfloat16 [2048, 256], P(('cam', 'tile'))
- grad_values: bfloat16 [2048, 256], P(('cam', 'tile'))
Inputs may be any that keep to these rules, and one draw needn't show every extreme that they name: Every tile has at least one visible block. `queries`: projected query features. `keys`: projected key features.
All inputs are finite; a program needn't handle non-finite values.
Results may differ from a plain program's by a relative error of at most 0.0052.
Values may be sent and summed in bfloat16 or wider, within the bound.
No kernel may reach another device: no remote copies, remote signals or barrier semaphores. Data moves between devices by JAX's collectives and lax.ppermute only.
A program may use at most 128 MiB of HBM per device.

v0:
```python
import math
import jax
import jax.numpy as jnp
from jax import lax
from jax.sharding import PartitionSpec as P

H = 8


def merged(array, axis, combine):
    everything = jax.tree.map(lambda part: lax.all_gather(part, axis), array)
    initial = jax.tree.map(lambda part: part[0], everything)

    def step(k, so_far):
        return combine(so_far, jax.tree.map(lambda part: part[k], everything))

    return lax.fori_loop(1, lax.axis_size(axis), step, initial)


def combine_stats(first, second):
    top = jnp.maximum(first[0], second[0])
    total = first[1] * jnp.exp(first[0] - top) + second[1] * jnp.exp(second[0] - top)
    return (top, total)


def shards(queries, keys, values, grad_out, visible, counts):
    row_count, width = queries.shape
    head_dim = width // H
    scale = 1.0 / math.sqrt(head_dim)
    key_all, value_all = (
        lax.all_gather(keys, "tile", axis=0, tiled=True),
        lax.all_gather(values, "tile", axis=0, tiled=True),
    )
    group = key_all.shape[0]
    block_count = counts.shape[0]
    block_keys = group // block_count
    slot_index = jnp.arange(group, dtype=jnp.int32) % block_keys
    key_valid = slot_index < jnp.repeat(counts, block_keys)
    tile_count = visible.shape[0]
    tile_rows = row_count // tile_count
    mask_tiles = (jnp.repeat(visible, block_keys, axis=1) == 1) & key_valid[None, :]
    per_step = 2
    step_count = tile_count // per_step
    step_rows = per_step * tile_rows
    query_blocks = queries.reshape(step_count, step_rows, H, head_dim)
    grad_blocks = grad_out.reshape(step_count, step_rows, H, head_dim)
    mask_blocks = mask_tiles.reshape(step_count, per_step, group)
    key_heads = key_all.reshape(group, H, head_dim)
    value_heads = value_all.reshape(group, H, head_dim)

    def scores_of(query_blk, key_mat):
        return (
            jnp.einsum("qhd,khd->hqk", query_blk, key_mat, preferred_element_type=jnp.float32)
            * scale
        )

    def row_mask(mask_blk):
        return jnp.repeat(mask_blk, tile_rows, axis=0)[None, :, :]

    def local_stats(inputs):
        query_blk, mask_blk = inputs
        scores = scores_of(query_blk, key_heads)
        allowed = row_mask(mask_blk)
        top = jnp.max(jnp.where(allowed, scores, -1e30), axis=-1)
        total = jnp.sum(jnp.where(allowed, jnp.exp(scores - top[..., None]), 0.0), axis=-1)
        return (top, total)

    local_top, local_total = lax.map(local_stats, (query_blocks, mask_blocks))
    global_top, global_total = merged((local_top, local_total), "cam", combine_stats)
    lse_all = global_top + jnp.log(global_total)

    def probs_terms(query_blk, grad_blk, mask_blk, lse_blk, key_mat, value_mat):
        scores = scores_of(query_blk, key_mat)
        allowed = row_mask(mask_blk)
        probs = jnp.where(allowed, jnp.exp(scores - lse_blk[..., None]), 0.0)
        dprobs = jnp.einsum("qhd,khd->hqk", grad_blk, value_mat, preferred_element_type=jnp.float32)
        return (probs, dprobs)

    def local_delta(inputs):
        query_blk, grad_blk, mask_blk, lse_blk = inputs
        probs, dprobs = probs_terms(query_blk, grad_blk, mask_blk, lse_blk, key_heads, value_heads)
        return jnp.sum(probs * dprobs, axis=-1)

    delta_part = lax.map(local_delta, (query_blocks, grad_blocks, mask_blocks, lse_all))
    delta_all = lax.psum(delta_part, "cam")

    def rounded_terms(query_blk, grad_blk, mask_blk, lse_blk, delta_blk, key_mat, value_mat):
        probs, dprobs = probs_terms(query_blk, grad_blk, mask_blk, lse_blk, key_mat, value_mat)
        dscores = probs * (dprobs - delta_blk[..., None])
        return (probs.astype(jnp.bfloat16), dscores.astype(jnp.bfloat16))

    def query_grad_of(dscores_b):
        grad_q = (
            jnp.einsum("hqk,khd->qhd", dscores_b, key_heads, preferred_element_type=jnp.float32)
            * scale
        )
        return grad_q.reshape(step_rows, width)

    def grad_step(carry, inputs):
        query_blk, grad_blk, mask_blk, lse_blk, delta_blk = inputs
        probs_b, dscores_b = rounded_terms(
            query_blk, grad_blk, mask_blk, lse_blk, delta_blk, key_heads, value_heads
        )
        grad_k = (
            carry[0]
            + jnp.einsum("hqk,qhd->khd", dscores_b, query_blk, preferred_element_type=jnp.float32)
            * scale
        )
        grad_v = carry[1] + jnp.einsum(
            "hqk,qhd->khd", probs_b, grad_blk, preferred_element_type=jnp.float32
        )
        return ((grad_k, grad_v), query_grad_of(dscores_b))

    zero_kv = jnp.zeros((group, H, head_dim), jnp.float32)
    (grad_k, grad_v), query_parts = lax.scan(
        grad_step, (zero_kv, zero_kv), (query_blocks, grad_blocks, mask_blocks, lse_all, delta_all)
    )
    joined = jnp.concatenate((grad_k.reshape(group, width), grad_v.reshape(group, width)), axis=1)
    owned = lax.psum_scatter(joined, "tile", scatter_dimension=0, tiled=True)
    grad_queries = lax.psum(query_parts.reshape(row_count, width), "cam").astype(jnp.bfloat16)
    grad_keys = owned[:, :width].astype(jnp.bfloat16)
    grad_values = owned[:, width:].astype(jnp.bfloat16)
    return (grad_queries, grad_keys, grad_values)


def solution(mesh):
    in_specs = (
        P("tile", None),
        P(("cam", "tile"), None),
        P(("cam", "tile"), None),
        P("tile", None),
        P("tile", "cam"),
        P("cam"),
    )
    out_specs = (P("tile", None), P(("cam", "tile"), None), P(("cam", "tile"), None))
    return jax.shard_map(shards, mesh=mesh, in_specs=in_specs, out_specs=out_specs, check_vma=False)
```

profile of v0, /device:TPU:0, one launch (start us, length us, event | category | flops | bytes accessed | tf_op | source)
XLA Modules:
  0.0 218.7 jit_solution(8810301855245995741)
XLA Ops:
  7.2 0.7 broadcast_in_dim.79
  8.0 0.7 broadcast_compare_fusion
  8.9 45.6 %all_gather.18 = bf16[1024,256]{1,0:T(8,128)(2,1)S(1)} all-gather(bf16[64,256]{1,0:T(8,128)(2,1)} %param.7), channel_id=1, replica_groups=mesh['cam'=2,'tile'=16] {'tile'}, dimensions={0}, use_global_device_ids=true | all-gather | bytes 557056 | tf_op jit(solution)/shard_map/all_gather | solution.py:31
  54.7 1.0 copy.18
  55.8 1.7 select_reduce_fusion.1
  57.5 1.8 all-gather
  59.3 1.4 copy-done
  60.7 2.4 %select_reduce_fusion = f32[8,256]{1,0:T(8,128)S(1)} fusion(f32[8,256,1024]{2,1,0:T(8,128)S(1)} %get-tuple-element.69, f32[8,256]{1,0:T(8,128)S(1)} %get-tuple-element.68, pred[256,1024]{1,0:T(8,128)(4,1)S(1)} %bitcast.24), kind=kLoop, calls=%fused_computation.3 | loop fusion | flops 8386560 | bytes 8667136 | tf_op jit(solution)/shard_map/while/body/eval_jaxpr/reduce_sum | solution.py:65
  63.1 1.8 all-gather.1
  65.1 38.3 %all_gather.23 = bf16[1024,256]{1,0:T(8,128)(2,1)S(1)} all-gather(bf16[64,256]{1,0:T(8,128)(2,1)S(1)} %copy-done.4), channel_id=1, replica_groups=mesh['cam'=2,'tile'=16] {'tile'}, dimensions={0}, use_global_device_ids=true | all-gather | bytes 557056 | tf_op jit(solution)/shard_map/all_gather | solution.py:32
  103.6 5.7 %fusion.1 = f32[8,1024,32]{1,2,0:T(8,128)} fusion(bf16[256,8,32]{0,2,1:T(8,128)(2,1)S(1)} %bitcast.36, f32[8,256,1024]{2,1,0:T(8,128)} %copy-done, f32[8,256]{1,0:T(8,128)S(1)} %fusion.6, pred[256,1024]{1,0:T(8,128)(4,1)S(1)} %bitcast.25), kind=kOutput, calls=%fused_computation.6 | convolution fusion | flops 142606336 | bytes 9838592 | tf_op jit(solution)/shard_map/while/body/eval_jaxpr/hqk,qhd->khd/dot_general | solution.py:109
  109.6 5.4 %multiply_reduce_fusion = (f32[8,256]{1,0:T(8,128)S(1)}, f32[8,256,1024]{2,1,0:T(8,128)}) fusion(f32[8,256,1024]{2,1,0:T(8,128)S(1)} %copy-done.1, f32[8,256]{1,0:T(8,128)S(1)} %fusion.6, pred[256,1024]{1,0:T(8,128)(4,1)S(1)} %bitcast.26, bf16[256,8,32]{0,2,1:T(8,128)(2,1)S(1)} %bitcast.37, bf16[1024,8,32]{0,2,1:T(8,128)(2,1)S(1)} %bitcast.31), kind=kOutput, calls=%fused_computation.1 | convolution fusion | flops 144701440 | bytes 17711104 | tf_op jit(solution)/shard_map/while/body/eval_jaxpr/qhd,khd->hqk/dot_general | solution.py:76
  114.9 2.5 %psum.14 = f32[8,256]{1,0:T(8,128)S(1)} all-reduce(f32[8,256]{1,0:T(8,128)S(1)} %get-tuple-element.70), channel_id=1, replica_groups=mesh['cam'=2,'tile'=16] {'cam'}, use_global_device_ids=true, to_apply=%region_3.4 | all-reduce | flops 2048 | bytes 16384 | tf_op jit(solution)/shard_map/psum | solution.py:85
  117.4 7.1 %multiply_convert_fusion = bf16[8,256,1024]{2,1,0:T(8,128)(2,1)S(1)} fusion(f32[8,256,1024]{2,1,0:T(8,128)} %get-tuple-element.71, f32[8,256,1024]{2,1,0:T(8,128)} %copy-done, f32[8,256]{1,0:T(8,128)S(1)} %psum.14, f32[8,256]{1,0:T(8,128)S(1)} %fusion.6, pred[256,1024]{1,0:T(8,128)(4,1)S(1)} %bitcast.27), kind=kLoop, calls=%fused_computation | loop fusion | flops 12582912 | bytes 21250048 | tf_op jit(solution)/shard_map/while/body/eval_jaxpr/convert_element_type | solution.py:90
  124.5 1.9 copy-done.2
  126.4 0.8 convolution_multiply_fusion
  127.2 0.3 copy.23
  127.6 1.6 copy.24
  129.1 1.7 pad_maximum_fusion
  130.8 3.5 %convolution_multiply_fusion.1 = f32[8,256,32]{1,2,0:T(8,128)S(1)} fusion(bf16[8,256,1024]{2,1,0:T(8,128)(2,1)} %copy-done.2, bf16[1024,8,32]{0,2,1:T(8,128)(2,1)S(1)} %bitcast.29), kind=kOutput, calls=%fused_computation.10 | convolution fusion | flops 134283264 | bytes 4980736 | tf_op jit(solution)/shard_map/while/body/eval_jaxpr/hqk,khd->qhd/dot_general | solution.py:94
  134.5 4.7 %all-reduce.1 = bf16[256,256]{1,0:T(8,128)(2,1)} all-reduce(f32[256,256]{1,0:T(8,128)S(1)} %copy.22), channel_id=1, replica_groups=mesh['cam'=2,'tile'=16] {'cam'}, use_global_device_ids=true, to_apply=%region_4.5 | all-reduce | flops 65536 | bytes 393216 | tf_op jit(solution)/shard_map/psum | solution.py:120
  139.2 71.1 %reduce-scatter.2.cloned.1.call-done = f32[64,512]{1,0:T(8,128)} async-done(((f32[1024,512]{1,0:T(8,128)}), f32[64,512]{1,0:T(8,128)}) %reduce-scatter.2.cloned.1.call-update) | async-done | bytes 131088 | tf_op jit(solution)/shard_map/reduce_scatter | solution.py:119
  210.3 0.9 convert.4
  211.2 0.6 fusion.14
  (21 shorter events, 1.4 us)
Async XLA Ops:
  7.2 203.2 %reduce-scatter.2.cloned.1.call-start = ((), (), s32[]{:S(2)}) async-start(), calls=%async_computation.1 | async-start | bytes 2228224 | tf_op jit(solution)/shard_map/reduce_scatter | solution.py:119
  55.8 9.2 %copy-start.3 = (bf16[256,256]{1,0:T(8,128)(2,1)S(1)}, bf16[256,256]{1,0:T(8,128)(2,1)}, u32[]{:S(2)}) copy-start(bf16[256,256]{1,0:T(8,128)(2,1)} %param.9) | copy-start | bytes 393220
  55.8 9.3 %copy-start.4 = (bf16[64,256]{1,0:T(8,128)(2,1)S(1)}, bf16[64,256]{1,0:T(8,128)(2,1)}, u32[]{:S(2)}) copy-start(bf16[64,256]{1,0:T(8,128)(2,1)} %param.8) | copy-start | bytes 98308
  57.5 3.2 %copy-start = (f32[8,256,1024]{2,1,0:T(8,128)}, f32[8,256,1024]{2,1,0:T(8,128)S(1)}, u32[]{:S(2)}) copy-start(f32[8,256,1024]{2,1,0:T(8,128)S(1)} %get-tuple-element.69) | copy-start | bytes 25165828
  103.5 6.0 %copy-start.1 = (f32[8,256,1024]{2,1,0:T(8,128)S(1)}, f32[8,256,1024]{2,1,0:T(8,128)}, u32[]{:S(2)}) copy-start(f32[8,256,1024]{2,1,0:T(8,128)} %copy-done) | copy-start | bytes 25165828
  124.5 1.9 copy-start.2
Sparse Core Ops, SparseCore 0:
  130.9 79.3 reduce-scatter.1
where the time goes:
time: 219 us
  blocking collectives  94.6 us (43%)
  waiting for transfers between devices  71.2 us (33%)
  matrix products  17.1 us (8%)
  between operations  14.2 us (6%)
  other arithmetic  12.8 us (6%)
  local copies, waits for them, and re-layouts  8.84 us (4%)
    reduce_scatter x1, waiting for transfers between devices, shards(): owned = lax.psum_scatter(joined, 'tile', scatter_dimension=0, tiled=True)  71.1 us
    all_gather x1, blocking collectives, shards(): lax.all_gather(keys, 'tile', axis=0, tiled=True)  45.6 us
    all_gather x1, blocking collectives, shards(): lax.all_gather(values, 'tile', axis=0, tiled=True)  38.3 us
    convert_element_type x1, other arithmetic, rounded_terms(): return (probs.astype(jnp.bfloat16), dscores.astype(jnp.bfloat16))  7.09 us
    dot_general x1, matrix products, grad_step(): jnp.einsum('hqk,qhd->khd', probs_b, grad_blk, preferred_element_type=jnp....  5.71 us
    dot_general x1, matrix products, probs_terms(): jnp.einsum('qhd,khd->hqk', grad_blk, value_mat, preferred_element_type=jn...  5.35 us
    unnamed x12, local copies, waits for them, and re-layouts  4.72 us
    psum x1, blocking collectives, shards(): lax.psum(query_parts.reshape(row_count, width), 'cam').astype(jnp.bfloat16)  4.69 us
  transfers between devices with their start and end apart: 1, of which 1 were waited for; matrix products, arithmetic and copies ran while one was open for 2% of the time, Pallas kernels for 0%

commit v1 on v0

--- a/solution.py
+++ b/solution.py
@@ -1,3 +1,4 @@
+import functools
 import math
 import jax
 import jax.numpy as jnp
@@ -5,6 +6,34 @@
 from jax.sharding import PartitionSpec as P
 
 H = 8
+
+
+def slabs_unite(state, pos_dim):
+    spare, piece_out, answer = (lax.axis_size("tile"), lax.axis_index("tile"), state.shape[pos_dim])
+    log = tuple(((tick, (tick + 1) % spare) for tick in range(spare)))
+    ledger = tuple(((tick, (tick - 1) % spare) for tick in range(spare)))
+    r2 = jnp.zeros(
+        (*state.shape[:pos_dim], spare * answer, *state.shape[pos_dim + 1 :]), state.dtype
+    )
+    r2 = lax.dynamic_update_slice_in_dim(r2, state, piece_out * answer, axis=pos_dim)
+    row_out = ready = state
+    current_arr = spare // 2
+    p = 1
+    while p < current_arr + 1:
+        row_out = lax.ppermute(row_out, axis_name="tile", perm=log)
+        r2 = lax.dynamic_update_slice_in_dim(
+            r2, row_out, (piece_out - p) % spare * answer, axis=pos_dim
+        )
+        if p < spare - current_arr:
+            ready = lax.ppermute(ready, axis_name="tile", perm=ledger)
+            r2 = lax.dynamic_update_slice_in_dim(
+                r2, ready, (piece_out + p) % spare * answer, axis=pos_dim
+            )
+        p = p + 1
+    return r2
+
+
+frames_replace = functools.partial(slabs_unite, pos_dim=0)
 
 
 def merged(array, axis, combine):
@@ -27,10 +56,7 @@
     row_count, width = queries.shape
     head_dim = width // H
     scale = 1.0 / math.sqrt(head_dim)
-    key_all, value_all = (
-        lax.all_gather(keys, "tile", axis=0, tiled=True),
-        lax.all_gather(values, "tile", axis=0, tiled=True),
-    )
+    key_all, value_all = (frames_replace(keys), lax.all_gather(values, "tile", axis=0, tiled=True))
     group = key_all.shape[0]
     block_count = counts.shape[0]
     block_keys = group // block_count

time: 219 us -> 235 us (1.073)
  blocking collectives: 94.6 us -> 55.3 us
  starting transfers between devices: 0.04 us -> 35.7 us
  waiting for transfers between devices: 71.2 us -> 85.3 us
  local copies, waits for them, and re-layouts: 8.84 us -> 18.1 us
  matrix products: 17.1 us -> 13.3 us
    all_gather x1 -> x0, blocking collectives: 45.6 us -> none  [shards(): lax.all_gather(keys, 'tile', axis=0, tiled=True)]
    ppermute x0 -> x15, starting transfers between devices: none -> 35.7 us  [the longest x7 30.6 us: slabs_unite(): ready = lax.ppermute(ready, axis_name='tile', perm=ledger)]
    ppermute x0 -> x15, waiting for transfers between devices: none -> 10.2 us  [the longest x8 7.62 us: slabs_unite(): row_out = lax.ppermute(row_out, axis_name='tile', perm=log)]
    dynamic_update_slice x0 -> x16, local copies, waits for them, and re-layouts: none -> 7.19 us  [the longest x8 3.55 us: slabs_unite(): lax.dynamic_update_slice_in_dim(r2, row_out, (piece_out - p) % spare * an...]
    all_gather x1, blocking collectives: 38.3 us -> 44.3 us  [shards(): lax.all_gather(values, 'tile', axis=0, tiled=True)]
    reduce_scatter x1, waiting for transfers between devices: 71.1 us -> 75.1 us  [shards(): owned = lax.psum_scatter(joined, 'tile', scatter_dimension=0, tiled=True)]
    dot_general x1, matrix products: 5.71 us -> 1.78 us  [grad_step(): jnp.einsum('hqk,qhd->khd', probs_b, grad_blk, preferred_element_type=jnp....]
    unnamed x12 -> x7, local copies, waits for them, and re-layouts: 4.72 us -> 4.82 us
  transfers between devices with their start and end apart: 1 -> 16, of which waited for: 1 -> 9; matrix products, arithmetic and copies ran while one was open for 2% -> 7% of each run, Pallas kernels for 0% -> 0%
where the time goes in v1:
time: 235 us
  waiting for transfers between devices  85.3 us (36%)
  blocking collectives  55.3 us (24%)
  starting transfers between devices  35.7 us (15%)
  local copies, waits for them, and re-layouts  18.1 us (8%)
  between operations  14.7 us (6%)
  matrix products  13.3 us (6%)
  other arithmetic  12 us (5%)
    reduce_scatter x1, waiting for transfers between devices, shards(): owned = lax.psum_scatter(joined, 'tile', scatter_dimension=0, tiled=True)  75.1 us
    all_gather x1, blocking collectives, shards(): lax.all_gather(values, 'tile', axis=0, tiled=True)  44.3 us
    ppermute x7, starting transfers between devices, slabs_unite(): ready = lax.ppermute(ready, axis_name='tile', perm=ledger)  30.6 us
    ppermute x8, waiting for transfers between devices, slabs_unite(): row_out = lax.ppermute(row_out, axis_name='tile', perm=log)  7.62 us
    convert_element_type x1, other arithmetic, rounded_terms(): return (probs.astype(jnp.bfloat16), dscores.astype(jnp.bfloat16))  7.03 us
    ppermute x8, starting transfers between devices, slabs_unite(): row_out = lax.ppermute(row_out, axis_name='tile', perm=log)  5.06 us
    unnamed x7, local copies, waits for them, and re-layouts  4.82 us
    dot_general x1, matrix products, probs_terms(): jnp.einsum('qhd,khd->hqk', grad_blk, value_mat, preferred_element_type=jn...  4.74 us
  transfers between devices with their start and end apart: 16, of which 9 were waited for; matrix products, arithmetic and copies ran while one was open for 7% of the time, Pallas kernels for 0%

profile of v1, /device:TPU:0, one launch (start us, length us, event | category | flops | bytes accessed | tf_op | source)
XLA Modules:
  0.0 234.5 jit_solution(3633510461998323467)
XLA Ops:
  7.2 3.0 %collective-permute-start = (bf16[64,256]{1,0:T(8,128)(2,1)}, bf16[64,256]{1,0:T(8,128)(2,1)S(1)}, u32[]{:S(2)}, u32[]{:S(2)}) collective-permute-start(bf16[64,256]{1,0:T(8,128)(2,1)} %param.7), channel_id=1, source_target_pairs={{0,1},{1,2},{2,3},{3,4},{4,5},{5,6},{6,7},{7,8},{8,9},{9,10},{10,1... | collective-permute-start | bytes 98312 | tf_op jit(solution)/shard_map/ppermute | solution.py:23
  10.2 4.1 %collective-permute-start.1 = (bf16[64,256]{1,0:T(8,128)(2,1)}, bf16[64,256]{1,0:T(8,128)(2,1)S(1)}, u32[]{:S(2)}, u32[]{:S(2)}) collective-permute-start(bf16[64,256]{1,0:T(8,128)(2,1)} %param.7), channel_id=1, source_target_pairs={{0,15},{1,0},{2,1},{3,2},{4,3},{5,4},{6,5},{7,6},{8,7},{9,8},{10,9... | collective-permute-start | bytes 98312 | tf_op jit(solution)/shard_map/ppermute | solution.py:28
  14.3 2.0 collective-permute-done
  16.3 5.7 %collective-permute-start.3 = (bf16[64,256]{1,0:T(8,128)(2,1)S(1)}, bf16[64,256]{1,0:T(8,128)(2,1)S(1)}, u32[]{:S(2)}, u32[]{:S(2)}) collective-permute-start(bf16[64,256]{1,0:T(8,128)(2,1)S(1)} %collective-permute-done.1), channel_id=1, source_target_pairs={{0,15},{1,0},{2,1},{3,2},{4,3},{5,4},{6,5},{7,6},{8,7},{9,8},{10,9... | collective-permute-start | bytes 98312 | tf_op jit(solution)/shard_map/ppermute | solution.py:28
  22.0 1.8 collective-permute-done.2
  23.8 5.7 %collective-permute-start.5 = (bf16[64,256]{1,0:T(8,128)(2,1)S(1)}, bf16[64,256]{1,0:T(8,128)(2,1)S(1)}, u32[]{:S(2)}, u32[]{:S(2)}) collective-permute-start(bf16[64,256]{1,0:T(8,128)(2,1)S(1)} %collective-permute-done.3), channel_id=1, source_target_pairs={{0,15},{1,0},{2,1},{3,2},{4,3},{5,4},{6,5},{7,6},{8,7},{9,8},{10,9... | collective-permute-start | bytes 98312 | tf_op jit(solution)/shard_map/ppermute | solution.py:28
  29.5 1.8 collective-permute-done.4
  31.4 5.7 %collective-permute-start.7 = (bf16[64,256]{1,0:T(8,128)(2,1)S(1)}, bf16[64,256]{1,0:T(8,128)(2,1)S(1)}, u32[]{:S(2)}, u32[]{:S(2)}) collective-permute-start(bf16[64,256]{1,0:T(8,128)(2,1)S(1)} %collective-permute-done.5), channel_id=1, source_target_pairs={{0,15},{1,0},{2,1},{3,2},{4,3},{5,4},{6,5},{7,6},{8,7},{9,8},{10,9... | collective-permute-start | bytes 98312 | tf_op jit(solution)/shard_map/ppermute | solution.py:28
  37.1 1.8 collective-permute-done.6
  38.9 44.3 %all_gather.19 = bf16[1024,256]{1,0:T(8,128)(2,1)S(1)} all-gather(bf16[64,256]{1,0:T(8,128)(2,1)} %param.8), channel_id=1, replica_groups=mesh['cam'=2,'tile'=16] {'tile'}, dimensions={0}, use_global_device_ids=true | all-gather | bytes 557056 | tf_op jit(solution)/shard_map/all_gather | solution.py:59
  84.0 2.0 collective-permute-start.10
  86.1 1.9 collective-permute-done.9
  87.9 3.6 %collective-permute-start.11 = (bf16[64,256]{1,0:T(8,128)(2,1)S(1)}, bf16[64,256]{1,0:T(8,128)(2,1)S(1)}, u32[]{:S(2)}, u32[]{:S(2)}) collective-permute-start(bf16[64,256]{1,0:T(8,128)(2,1)S(1)} %collective-permute-done.9), channel_id=1, source_target_pairs={{0,15},{1,0},{2,1},{3,2},{4,3},{5,4},{6,5},{7,6},{8,7},{9,8},{10,9... | collective-permute-start | bytes 98312 | tf_op jit(solution)/shard_map/ppermute | solution.py:28
  93.1 5.9 %collective-permute-start.13 = (bf16[64,256]{1,0:T(8,128)(2,1)S(1)}, bf16[64,256]{1,0:T(8,128)(2,1)S(1)}, u32[]{:S(2)}, u32[]{:S(2)}) collective-permute-start(bf16[64,256]{1,0:T(8,128)(2,1)S(1)} %collective-permute-done.11), channel_id=1, source_target_pairs={{0,15},{1,0},{2,1},{3,2},{4,3},{5,4},{6,5},{7,6},{8,7},{9,8},{10,9... | collective-permute-start | bytes 98312 | tf_op jit(solution)/shard_map/ppermute | solution.py:28
  113.8 2.0 all-gather
  117.5 1.8 all-gather.1
  121.1 4.7 %multiply_reduce_fusion = (f32[8,256]{1,0:T(8,128)S(1)}, f32[8,256,1024]{1,2,0:T(8,128)}) fusion(f32[8,1024,256]{2,1,0:T(8,128)S(1)} %get-tuple-element.69, f32[8,256]{1,0:T(8,128)S(1)} %fusion.12, pred[256,1024]{0,1:T(8,128)(4,1)S(1)} %copy.55, bf16[256,8,32]{0,2,1:T(8,128)(2,1)S(1)} %bitcast.56, bf16[1024,8,32]{0,2,1:T(8,128)(2,1)S(1)} %bitcast.49), kind=kOutput, calls=%fused_computation.10 | convolution fusion | flops 144701440 | bytes 17711104 | tf_op jit(solution)/shard_map/while/body/eval_jaxpr/qhd,khd->hqk/dot_general | solution.py:102
  125.9 2.5 %psum.14 = f32[8,256]{1,0:T(8,128)S(1)} all-reduce(f32[8,256]{1,0:T(8,128)S(1)} %get-tuple-element.70), channel_id=1, replica_groups=mesh['cam'=2,'tile'=16] {'cam'}, use_global_device_ids=true, to_apply=%region_3.4 | all-reduce | flops 2048 | bytes 16384 | tf_op jit(solution)/shard_map/psum | solution.py:111
  128.7 7.0 %multiply_convert_fusion = bf16[8,256,1024]{1,2,0:T(8,128)(2,1)S(1)} fusion(f32[8,256,1024]{1,2,0:T(8,128)} %get-tuple-element.71, f32[8,1024,256]{2,1,0:T(8,128)} %copy-done, f32[8,256]{1,0:T(8,128)S(1)} %psum.14, f32[8,256]{1,0:T(8,128)S(1)} %fusion.12, pred[256,1024]{0,1:T(8,128)(4,1)S(1)} %copy.55), kind=kLoop, calls=%fused_computation.9 | loop fusion | flops 12582912 | bytes 21250048 | tf_op jit(solution)/shard_map/while/body/eval_jaxpr/convert_element_type | solution.py:116
  135.7 1.9 copy-done.1
  137.7 2.3 convolution_multiply_fusion
  143.2 3.0 %convolution_multiply_fusion.1 = f32[8,32,256]{2,1,0:T(8,128)S(1)} fusion(bf16[1024,8,32]{0,2,1:T(8,128)(2,1)S(1)} %bitcast.47, bf16[8,256,1024]{1,2,0:T(8,128)(2,1)} %copy-done.1), kind=kOutput, calls=%fused_computation.16 | convolution fusion | flops 134283264 | bytes 4980736 | tf_op jit(solution)/shard_map/while/body/eval_jaxpr/hqk,khd->qhd/dot_general | solution.py:120
  146.3 4.7 %all-reduce.1 = bf16[256,256]{1,0:T(8,128)(2,1)} all-reduce(f32[256,256]{1,0:T(8,128)S(1)} %copy.62), channel_id=1, replica_groups=mesh['cam'=2,'tile'=16] {'cam'}, use_global_device_ids=true, to_apply=%region_4.5 | all-reduce | flops 65536 | bytes 393216 | tf_op jit(solution)/shard_map/psum | solution.py:146
  151.0 75.1 %reduce-scatter.2.cloned.1.call-done = f32[64,512]{1,0:T(8,128)} async-done(((f32[1024,512]{1,0:T(8,128)}), f32[64,512]{1,0:T(8,128)}) %reduce-scatter.2.cloned.1.call-update) | async-done | bytes 131088 | tf_op jit(solution)/shard_map/reduce_scatter | solution.py:145
  (77 shorter events, 25.3 us)
Async XLA Ops:
  7.2 219.0 %reduce-scatter.2.cloned.1.call-start = ((), (), s32[]{:S(2)}) async-start(), calls=%async_computation.1 | async-start | bytes 2228224 | tf_op jit(solution)/shard_map/reduce_scatter | solution.py:145
  7.2 9.1 %collective-permute-start = (bf16[64,256]{1,0:T(8,128)(2,1)}, bf16[64,256]{1,0:T(8,128)(2,1)S(1)}, u32[]{:S(2)}, u32[]{:S(2)}) collective-permute-start(bf16[64,256]{1,0:T(8,128)(2,1)} %param.7), channel_id=1, source_target_pairs={{0,1},{1,2},{2,3},{3,4},{4,5},{5,6},{6,7},{7,8},{8,9},{9,10},{10,1... | collective-permute-start | bytes 98312 | tf_op jit(solution)/shard_map/ppermute | solution.py:23
  10.2 6.1 %collective-permute-start.1 = (bf16[64,256]{1,0:T(8,128)(2,1)}, bf16[64,256]{1,0:T(8,128)(2,1)S(1)}, u32[]{:S(2)}, u32[]{:S(2)}) collective-permute-start(bf16[64,256]{1,0:T(8,128)(2,1)} %param.7), channel_id=1, source_target_pairs={{0,15},{1,0},{2,1},{3,2},{4,3},{5,4},{6,5},{7,6},{8,7},{9,8},{10,9... | collective-permute-start | bytes 98312 | tf_op jit(solution)/shard_map/ppermute | solution.py:28
  16.3 7.5 %collective-permute-start.2 = (bf16[64,256]{1,0:T(8,128)(2,1)S(1)}, bf16[64,256]{1,0:T(8,128)(2,1)S(1)}, u32[]{:S(2)}, u32[]{:S(2)}) collective-permute-start(bf16[64,256]{1,0:T(8,128)(2,1)S(1)} %collective-permute-done), channel_id=1, source_target_pairs={{0,1},{1,2},{2,3},{3,4},{4,5},{5,6},{6,7},{7,8},{8,9},{9,10},{10,1... | collective-permute-start | bytes 98312 | tf_op jit(solution)/shard_map/ppermute | solution.py:23
  16.3 7.5 %collective-permute-start.3 = (bf16[64,256]{1,0:T(8,128)(2,1)S(1)}, bf16[64,256]{1,0:T(8,128)(2,1)S(1)}, u32[]{:S(2)}, u32[]{:S(2)}) collective-permute-start(bf16[64,256]{1,0:T(8,128)(2,1)S(1)} %collective-permute-done.1), channel_id=1, source_target_pairs={{0,15},{1,0},{2,1},{3,2},{4,3},{5,4},{6,5},{7,6},{8,7},{9,8},{10,9... | collective-permute-start | bytes 98312 | tf_op jit(solution)/shard_map/ppermute | solution.py:28
  23.8 7.5 %collective-permute-start.4 = (bf16[64,256]{1,0:T(8,128)(2,1)S(1)}, bf16[64,256]{1,0:T(8,128)(2,1)S(1)}, u32[]{:S(2)}, u32[]{:S(2)}) collective-permute-start(bf16[64,256]{1,0:T(8,128)(2,1)S(1)} %collective-permute-done.2), channel_id=1, source_target_pairs={{0,1},{1,2},{2,3},{3,4},{4,5},{5,6},{6,7},{7,8},{8,9},{9,10},{10,1... | collective-permute-start | bytes 98312 | tf_op jit(solution)/shard_map/ppermute | solution.py:23
  23.8 7.5 %collective-permute-start.5 = (bf16[64,256]{1,0:T(8,128)(2,1)S(1)}, bf16[64,256]{1,0:T(8,128)(2,1)S(1)}, u32[]{:S(2)}, u32[]{:S(2)}) collective-permute-start(bf16[64,256]{1,0:T(8,128)(2,1)S(1)} %collective-permute-done.3), channel_id=1, source_target_pairs={{0,15},{1,0},{2,1},{3,2},{4,3},{5,4},{6,5},{7,6},{8,7},{9,8},{10,9... | collective-permute-start | bytes 98312 | tf_op jit(solution)/shard_map/ppermute | solution.py:28
  31.4 7.5 %collective-permute-start.6 = (bf16[64,256]{1,0:T(8,128)(2,1)S(1)}, bf16[64,256]{1,0:T(8,128)(2,1)S(1)}, u32[]{:S(2)}, u32[]{:S(2)}) collective-permute-start(bf16[64,256]{1,0:T(8,128)(2,1)S(1)} %collective-permute-done.4), channel_id=1, source_target_pairs={{0,1},{1,2},{2,3},{3,4},{4,5},{5,6},{6,7},{7,8},{8,9},{9,10},{10,1... | collective-permute-start | bytes 98312 | tf_op jit(solution)/shard_map/ppermute | solution.py:23
  31.4 52.7 %collective-permute-start.7 = (bf16[64,256]{1,0:T(8,128)(2,1)S(1)}, bf16[64,256]{1,0:T(8,128)(2,1)S(1)}, u32[]{:S(2)}, u32[]{:S(2)}) collective-permute-start(bf16[64,256]{1,0:T(8,128)(2,1)S(1)} %collective-permute-done.5), channel_id=1, source_target_pairs={{0,15},{1,0},{2,1},{3,2},{4,3},{5,4},{6,5},{7,6},{8,7},{9,8},{10,9... | collective-permute-start | bytes 98312 | tf_op jit(solution)/shard_map/ppermute | solution.py:28
  38.9 45.1 %collective-permute-start.8 = (bf16[64,256]{1,0:T(8,128)(2,1)S(1)}, bf16[64,256]{1,0:T(8,128)(2,1)S(1)}, u32[]{:S(2)}, u32[]{:S(2)}) collective-permute-start(bf16[64,256]{1,0:T(8,128)(2,1)S(1)} %collective-permute-done.6), channel_id=1, source_target_pairs={{0,1},{1,2},{2,3},{3,4},{4,5},{5,6},{6,7},{7,8},{8,9},{9,10},{10,1... | collective-permute-start | bytes 98312 | tf_op jit(solution)/shard_map/ppermute | solution.py:23
  84.0 3.9 %collective-permute-start.9 = (bf16[64,256]{1,0:T(8,128)(2,1)S(1)}, bf16[64,256]{1,0:T(8,128)(2,1)S(1)}, u32[]{:S(2)}, u32[]{:S(2)}) collective-permute-start(bf16[64,256]{1,0:T(8,128)(2,1)S(1)} %collective-permute-done.7), channel_id=1, source_target_pairs={{0,15},{1,0},{2,1},{3,2},{4,3},{5,4},{6,5},{7,6},{8,7},{9,8},{10,9... | collective-permute-start | bytes 98312 | tf_op jit(solution)/shard_map/ppermute | solution.py:28
  84.0 7.6 %collective-permute-start.10 = (bf16[64,256]{1,0:T(8,128)(2,1)S(1)}, bf16[64,256]{1,0:T(8,128)(2,1)S(1)}, u32[]{:S(2)}, u32[]{:S(2)}) collective-permute-start(bf16[64,256]{1,0:T(8,128)(2,1)S(1)} %collective-permute-done.8), channel_id=1, source_target_pairs={{0,1},{1,2},{2,3},{3,4},{4,5},{5,6},{6,7},{7,8},{8,9},{9,10},{10,1... | collective-permute-start | bytes 98312 | tf_op jit(solution)/shard_map/ppermute | solution.py:23
  87.9 5.2 %collective-permute-start.11 = (bf16[64,256]{1,0:T(8,128)(2,1)S(1)}, bf16[64,256]{1,0:T(8,128)(2,1)S(1)}, u32[]{:S(2)}, u32[]{:S(2)}) collective-permute-start(bf16[64,256]{1,0:T(8,128)(2,1)S(1)} %collective-permute-done.9), channel_id=1, source_target_pairs={{0,15},{1,0},{2,1},{3,2},{4,3},{5,4},{6,5},{7,6},{8,7},{9,8},{10,9... | collective-permute-start | bytes 98312 | tf_op jit(solution)/shard_map/ppermute | solution.py:28
  91.6 7.5 %collective-permute-start.12 = (bf16[64,256]{1,0:T(8,128)(2,1)S(1)}, bf16[64,256]{1,0:T(8,128)(2,1)S(1)}, u32[]{:S(2)}, u32[]{:S(2)}) collective-permute-start(bf16[64,256]{1,0:T(8,128)(2,1)S(1)} %collective-permute-done.10), channel_id=1, source_target_pairs={{0,1},{1,2},{2,3},{3,4},{4,5},{5,6},{6,7},{7,8},{8,9},{9,10},{10,1... | collective-permute-start | bytes 98312 | tf_op jit(solution)/shard_map/ppermute | solution.py:23
  93.1 18.0 %collective-permute-start.13 = (bf16[64,256]{1,0:T(8,128)(2,1)S(1)}, bf16[64,256]{1,0:T(8,128)(2,1)S(1)}, u32[]{:S(2)}, u32[]{:S(2)}) collective-permute-start(bf16[64,256]{1,0:T(8,128)(2,1)S(1)} %collective-permute-done.11), channel_id=1, source_target_pairs={{0,15},{1,0},{2,1},{3,2},{4,3},{5,4},{6,5},{7,6},{8,7},{9,8},{10,9... | collective-permute-start | bytes 98312 | tf_op jit(solution)/shard_map/ppermute | solution.py:28
  99.1 12.7 %collective-permute-start.14 = (bf16[64,256]{1,0:T(8,128)(2,1)S(1)}, bf16[64,256]{1,0:T(8,128)(2,1)S(1)}, u32[]{:S(2)}, u32[]{:S(2)}) collective-permute-start(bf16[64,256]{1,0:T(8,128)(2,1)S(1)} %collective-permute-done.12), channel_id=1, source_target_pairs={{0,1},{1,2},{2,3},{3,4},{4,5},{5,6},{6,7},{7,8},{8,9},{9,10},{10,1... | collective-permute-start | bytes 98312 | tf_op jit(solution)/shard_map/ppermute | solution.py:23
  113.8 7.4 %copy-start = (f32[8,1024,256]{2,1,0:T(8,128)}, f32[8,1024,256]{2,1,0:T(8,128)S(1)}, u32[]{:S(2)}) copy-start(f32[8,1024,256]{2,1,0:T(8,128)S(1)} %get-tuple-element.69) | copy-start | bytes 25165828
  135.7 1.9 copy-start.1
Sparse Core Ops, SparseCore 0:
  143.3 82.7 reduce-scatter.1
